TPU v7x, 32 devices: a whole 2x2x4 slice. The times are simulated.
32 devices in a mesh: groups: 2 (over x), seq: 16 (over z, y, core).
Axes of the slice: x: 2, y: 2, z: 4, core: 2. Of those that a mesh axis runs over, the one named last changes fastest.
Arguments:
- queries: bfloat16 [96, 8192], P(('groups', 'seq')), parts along dimension 0, may hold values from -48 to 48
- prompt_of: int32 [96, 1], P(('groups', 'seq')), parts along dimension 0, may hold values from 0 to 1; in each aligned block of 3 rows (0 to 2, 3 to 5, ...) at most 2 rows name the same one
- suffix_cache: bfloat16 [96, 512, 2048], P(('groups', 'seq')), parts along dimension 0, may hold values from -6 to 6
- suffix_blocks: int32 [96], P(('groups', 'seq')), parts along dimension 0, may hold values from 1 to 4
- prompt_cache: bfloat16 [4, 2048, 2048], P('groups', 'seq'), parts along dimension 0, may hold values from -16 to 16
- reward_weight: float32 [8192], replicated, may hold values from -0.4375 to 0.4375
Outputs:
- attended: bfloat16 [96, 8192], P(('groups', 'seq')), parts along dimension 0
- scores: float32 [96], P(('groups', 'seq')), parts along dimension 0
There are 2 independent parts, one for each index of `groups`. A program takes and returns all parts, laid end to end along the dimension named above; an argument that names none is the same for every part. Nothing has to cross between parts.
Inputs may be any that keep to these rules, and one draw needn't show every extreme that they name: `prompt_of`: in each device's aligned block of 3 rows at most 2 candidates name the same prompt.
All inputs are finite; a program needn't handle non-finite values.
Results may differ from a plain program's by a relative error of at most 0.015.
Values may be sent and summed in bfloat16 or wider, within the bound.
No kernel may reach another device: no remote copies, remote signals or barrier semaphores. Data moves between devices by JAX's collectives and lax.ppermute only.
A program may use at most 192 MiB of HBM per device.

v0:
```python
import math

import jax
import jax.numpy as jnp
from jax import lax
from jax.experimental import pallas as pl
from jax.experimental.pallas import tpu as pltpu
from jax.sharding import PartitionSpec as P


HD = 128
BLOCK = 128
LOG2E = 1.4426950408889634

SLAB = 4
F32 = jnp.float32
BF16 = jnp.bfloat16
floor_logit = -1e30


def vmem_spec():
    return pl.BlockSpec(memory_space=pltpu.VMEM)


def near(arrays):
    return [pltpu.with_memory_space_constraint(x, pltpu.VMEM) for x in arrays]


def split3(x):
    high = x.astype(BF16).astype(F32)
    rest = x - high
    middle = rest.astype(BF16).astype(F32)
    low = (rest - middle).astype(BF16).astype(F32)
    return [high, middle, low]


def pack_stats(pairs):
    rows = []
    for shift, total in pairs:
        rows += [shift] + split3(total)
    rows += [jnp.zeros((1, HD), F32)] * (stat_rows(len(pairs)) - len(rows))
    return jnp.concatenate(rows, axis=0)


def stat_rows(kvq):
    return -(-4 * kvq // 8) * 8


def unpack_stats(stats, k):
    at = 4 * k
    total = stats[at + 1 : at + 2] + stats[at + 2 : at + 3] + stats[at + 3 : at + 4]
    return stats[at : at + 1], total


def to_lanes(column):
    rows = column.shape[0]
    same = lax.broadcasted_iota(jnp.int32, (rows, HD), 0) == lax.broadcasted_iota(
        jnp.int32, (rows, HD), 1
    )
    return jnp.sum(jnp.where(same, jnp.broadcast_to(column, (rows, HD)), 0.0), axis=0, keepdims=True)


def to_rows(lanes, rows, offset):
    same = lax.broadcasted_iota(jnp.int32, (rows, HD), 0) + offset == lax.broadcasted_iota(
        jnp.int32, (rows, HD), 1
    )
    return jnp.sum(jnp.where(same, jnp.broadcast_to(lanes, (rows, HD)), 0.0), axis=1, keepdims=True)


def prepare(queries, prompt_of, blocks, prompt_cache, kvq, group):
    cands, width = queries.shape
    heads = width // HD
    prompts, span, kv_width2 = prompt_cache.shape
    kv_width = kv_width2 // 2
    hq = kvq * group
    part_rows = kvq * cands * group + 8
    kvw = kvq * HD

    def kernel(q_hbm, ids_hbm, blocks_hbm, cache_ref, *rest):
        all_ref, live_ref, own_ref, near_ref, far_ref = rest[:5]
        kv_out = rest[5:7]
        q_ref, ids_ref, blocks_ref, scratch, sem, kv_sem = rest[7:]
        mine = lax.axis_index("seq") % SLAB
        copies = []
        for j in range(2):
            for side in range(2):
                column = pl.multiple_of(side * kv_width + (mine ^ (2 + j)) * kvw, kvw)
                copy = pltpu.make_async_copy(
                    cache_ref.at[:, :, pl.ds(column, kvw)], kv_out[j].at[side], kv_sem.at[j, side]
                )
                copy.start()
                copies.append(copy)
        q_copy = pltpu.make_async_copy(q_hbm, q_ref, sem.at[0])
        q_copy.start()
        ids_copy = pltpu.make_async_copy(ids_hbm, ids_ref, sem.at[1])
        ids_copy.start()
        blocks_copy = pltpu.make_async_copy(blocks_hbm, blocks_ref, sem.at[2])
        blocks_copy.start()
        q_copy.wait()
        for h in range(heads):
            scratch[pl.ds(h, cands, stride=heads), :] = q_ref[:, h * HD : (h + 1) * HD].astype(F32)
        all_ref[...] = scratch[...].astype(BF16)
        ids_copy.wait()
        blocks_copy.wait()
        for r in range(cands):
            live_ref[r : r + 1, :] = jnp.full((1, HD), BLOCK * blocks_ref[r])
        id_rows = [jnp.full((1, HD), ids_ref[r].astype(F32)) for r in range(cands)]
        id_rows = id_rows + [jnp.zeros((8 - cands, HD), F32)]
        for j in range(SLAB):
            first = (mine ^ j) * hq
            pieces = []
            for k in range(kvq):
                for r in range(cands):
                    at = pl.multiple_of(r * heads + first + k * group, 8)
                    pieces.append(scratch[pl.ds(at, group), :])
            part = jnp.concatenate(pieces + id_rows, axis=0).astype(BF16)
            if j < 2:
                (own_ref, near_ref)[j][...] = part
            else:
                far_ref[(j - 2) * part_rows : (j - 1) * part_rows, :] = part
        for copy in copies:
            copy.wait()

    hbm = pl.BlockSpec(memory_space=pl.ANY)
    out = pl.pallas_call(
        kernel,
        out_shape=[pltpu.VMEM((cands * heads, HD), BF16), pltpu.VMEM((8, HD), jnp.int32)]
        + [pltpu.VMEM((rows, HD), BF16) for rows in (part_rows, part_rows, 2 * part_rows)]
        + [pltpu.VMEM((2, prompts, span, kvw), BF16)] * 2,
        in_specs=[hbm] * 4,
        out_specs=[vmem_spec()] * 7,
        scratch_shapes=[
            pltpu.VMEM((cands, width), BF16),
            pltpu.SMEM((cands,), jnp.int32),
            pltpu.SMEM((cands,), jnp.int32),
            pltpu.VMEM((cands * heads, HD), F32),
            pltpu.SemaphoreType.DMA((3,)),
            pltpu.SemaphoreType.DMA((2, 2)),
        ],
        name="prepare",
    )(queries, prompt_of, blocks, prompt_cache)
    return out[0], out[1], out[2:5], out[5:]


def pack(own, near_part, far, passed):
    rows = own.shape[0]
    half = rows - 8

    def kernel(own_ref, near_ref, far_ref, passed_ref, out_ref):
        segment = lax.broadcasted_iota(jnp.int32, (8, HD), 1) // (HD // SLAB)
        ids = jnp.zeros((8, HD), F32)
        for j, (ref, at) in enumerate(((own_ref, 0), (near_ref, 0), (far_ref, 0), (passed_ref, rows))):
            out_ref[j * half : (j + 1) * half, :] = ref[at : at + half, :]
            ids = jnp.where(segment == j, ref[at + half : at + rows, :].astype(F32), ids)
        out_ref[SLAB * half :, :] = ids.astype(BF16)

    return pl.pallas_call(
        kernel,
        out_shape=pltpu.VMEM((SLAB * half + 8, HD), BF16),
        in_specs=[vmem_spec()] * 4,
        out_specs=vmem_spec(),
        name="pack",
    )(*near([own, near_part, far, passed]))


def suffix_attend(first, count, live, rows_q, suffix_cache, kv_heads, prompt_cache=None):
    cands, length, kv_width2 = suffix_cache.shape
    kv_width = kv_width2 // 2
    heads = rows_q.shape[0] // cands
    group = heads // kv_heads

    keeps = prompt_cache is not None
    if keeps:
        prompts, span, prompt_width2 = prompt_cache.shape
        prompt_width = prompt_width2 // 2
        kvw = prompt_width // SLAB

    def kernel(live_ref, q_ref, cache_ref, *rest):
        if keeps:
            prompt_ref, max_ref, sum_ref, mix_ref, *kv_refs, keys, values, sem, own_sem = rest
        else:
            max_ref, sum_ref, mix_ref, keys, values, sem = rest
        fetches = []
        for c in range(count):
            for side, target in enumerate((keys, values)):
                fetch = pltpu.make_async_copy(
                    cache_ref.at[first + c, :, side * kv_width : (side + 1) * kv_width],
                    target.at[c],
                    sem.at[c, side],
                )
                fetch.start()
                fetches.append(fetch)
        owns = []
        if keeps:
            mine = lax.axis_index("seq") % SLAB
            for j, ref in enumerate(kv_refs):
                for side in range(2):
                    column = pl.multiple_of(side * prompt_width + (mine ^ j) * kvw, kvw)
                    own = pltpu.make_async_copy(
                        prompt_ref.at[:, :, pl.ds(column, kvw)], ref.at[side], own_sem.at[j, side]
                    )
                    own.start()
                    owns.append(own)
        diagonal = (
            lax.broadcasted_iota(jnp.int32, (heads, kv_width), 0) // group
            == lax.broadcasted_iota(jnp.int32, (heads, kv_width), 1) // HD
        )
        position = lax.broadcasted_iota(jnp.int32, (heads, length), 1)
        for c in range(count):
            rows = slice(c * heads, (c + 1) * heads)
            held = first * heads
            wide = jnp.concatenate(
                [q_ref[held + c * heads : held + (c + 1) * heads, :]] * kv_heads, axis=1
            )
            wide = jnp.where(diagonal, wide, jnp.zeros_like(wide))
            fetches[2 * c].wait()
            logits = lax.dot_general(
                wide, keys[c], (((1,), (1,)), ((), ())), preferred_element_type=F32
            ) * (LOG2E * HD ** (-0.5))
            live_row = jnp.concatenate([live_ref[first + c : first + c + 1, :]] * (length // HD), axis=1)
            live = position < live_row
            logits = jnp.where(live, logits, floor_logit)
            maxima = jnp.max(logits, axis=1, keepdims=True)
            exponent = jnp.where(live, jnp.exp2(logits - maxima), 0.0)
            totals = jnp.sum(exponent, axis=1, keepdims=True)
            fetches[2 * c + 1].wait()
            mixed = jnp.dot(exponent.astype(BF16), values[c], preferred_element_type=F32)
            max_ref[rows, :] = jnp.broadcast_to(maxima, (heads, HD))
            sum_ref[rows, :] = jnp.broadcast_to(totals, (heads, HD))
            for k in range(kv_heads):
                at = c * heads + k * group
                mix_ref[at : at + group, :] = mixed[
                    k * group : (k + 1) * group, k * HD : (k + 1) * HD
                ]
        for own in owns:
            own.wait()

    hbm = pl.BlockSpec(memory_space=pl.ANY)
    extra = [pltpu.VMEM((2, prompts, span, kvw), BF16)] * 2 if keeps else []
    return pl.pallas_call(
        kernel,
        out_shape=[pltpu.VMEM((count * heads, HD), F32)] * 3 + extra,
        in_specs=[vmem_spec(), vmem_spec(), hbm] + [hbm] * keeps,
        out_specs=[vmem_spec()] * (3 + len(extra)),
        scratch_shapes=[
            pltpu.VMEM((count, length, kv_width), BF16),
            pltpu.VMEM((count, length, kv_width), BF16),
            pltpu.SemaphoreType.DMA((count, 2)),
        ]
        + [pltpu.SemaphoreType.DMA((2, 2))] * keeps,
        cost_estimate=pl.CostEstimate(
            flops=4 * count * heads * length * kv_width,
            transcendentals=count * heads * length,
            bytes_accessed=2 * suffix_cache.size * count // cands,
        ),
        name="suffix",
    )(*near([live, rows_q]), suffix_cache, *([prompt_cache] if keeps else []))


def prompt_attend(query_blocks, caches, cands, kvq, group):
    stacked = not isinstance(query_blocks, list)
    outer = query_blocks.shape[0] if stacked else len(query_blocks)
    chunk = math.gcd(outer, 4)
    part = cands * group
    part_rows = kvq * part
    block_rows = SLAB * part
    out_rows = kvq * block_rows + stat_rows(kvq)
    prompts, _ = caches[0].shape[1:3]

    def kernel(*refs):
        if stacked:
            q_refs = [refs[0].at[i] for i in range(chunk)]
            cache_refs = refs[1 : 1 + SLAB]
            out_refs = [refs[1 + SLAB].at[i] for i in range(chunk)]
        else:
            q_refs = refs[:chunk]
            cache_refs = refs[chunk : chunk + SLAB]
            out_refs = refs[chunk + SLAB :]
        rows = [q_ref[...].astype(F32) for q_ref in q_refs]
        ids = []
        segment = lax.broadcasted_iota(jnp.int32, (8, HD), 1) // (HD // SLAB)
        for i in range(chunk):
            for j in range(SLAB):
                mine = jnp.where(segment == j, rows[i][SLAB * part_rows :], 0.0)
                mine = jnp.max(mine, axis=1, keepdims=True)
                for r in range(cands):
                    ids.append(jnp.broadcast_to(mine[r : r + 1], (group, HD)))
        ids = jnp.concatenate(ids, axis=0)
        picked = [ids == float(p) for p in range(prompts)]
        stats = [[] for _ in range(chunk)]
        for k in range(kvq):
            q = jnp.concatenate(
                [
                    rows[i][j * part_rows + k * part : j * part_rows + (k + 1) * part]
                    for i in range(chunk)
                    for j in range(SLAB)
                ],
                axis=0,
            )
            q = jnp.concatenate([jnp.where(one, q, 0.0) for one in picked], axis=1).astype(BF16)

            def both(side):
                return jnp.concatenate(
                    [
                        jnp.concatenate(
                            [ref[side, p, :, k * HD : (k + 1) * HD] for p in range(prompts)], axis=1
                        )
                        for ref in cache_refs
                    ],
                    axis=0,
                )

            logits = lax.dot_general(
                q, both(0), (((1,), (1,)), ((), ())), preferred_element_type=F32
            ) * (LOG2E * HD ** (-0.5))
            maxima = jnp.max(logits, axis=1, keepdims=True).astype(BF16).astype(F32)
            exponent = jnp.exp2(logits - maxima)
            totals = jnp.sum(exponent, axis=1, keepdims=True)
            wide = jnp.dot(exponent.astype(BF16), both(1), preferred_element_type=F32)
            mixed = wide[:, :HD]
            for p in range(1, prompts):
                mixed = jnp.where(picked[p], wide[:, p * HD : (p + 1) * HD], mixed)
            for i in range(chunk):
                cut = slice(i * block_rows, (i + 1) * block_rows)
                out_refs[i][k * block_rows : (k + 1) * block_rows, :] = mixed[cut].astype(BF16)
                stats[i].append((to_lanes(maxima[cut]), to_lanes(totals[cut])))
        for i in range(chunk):
            out_refs[i][kvq * block_rows :, :] = pack_stats(stats[i]).astype(BF16)

    if stacked:
        whole = [
            pl.BlockSpec(c.shape, lambda s: (0, 0, 0, 0)) for c in caches
        ]
        return pl.pallas_call(
            kernel,
            out_shape=jax.ShapeDtypeStruct((outer, out_rows, HD), BF16),
            grid=(outer // chunk,),
            in_specs=[pl.BlockSpec((chunk, SLAB * part_rows + 8, HD), lambda s: (s, 0, 0))] + whole,
            out_specs=pl.BlockSpec((chunk, out_rows, HD), lambda s: (s, 0, 0)),
            name="prompt",
        )(query_blocks, *caches)
    return pl.pallas_call(
        kernel,
        out_shape=[pltpu.VMEM((out_rows, HD), BF16)] * outer,
        in_specs=[vmem_spec()] * (outer + SLAB),
        out_specs=[vmem_spec()] * outer,
        name="prompt",
    )(*near(query_blocks), *near(caches))


def merge(blocks, cands, kvq, group):
    stacked = not isinstance(blocks, list)
    outer = blocks.shape[0] if stacked else len(blocks)
    part = cands * group
    block_rows = SLAB * part
    out_rows = kvq * part + stat_rows(kvq)

    def kernel(*refs):
        if stacked:
            in_refs = [refs[0].at[i] for i in range(outer)]
            out_refs = refs[1:]
        else:
            in_refs = refs[:outer]
            out_refs = refs[outer:]
        stats = [ref[kvq * block_rows :, :].astype(F32) for ref in in_refs]
        merged = []
        for k in range(kvq):
            pairs = [unpack_stats(one, k) for one in stats]
            joined = pairs[0][0]
            for maximum, total in pairs[1:]:
                joined = jnp.maximum(joined, maximum)
            total_all = jnp.zeros((1, HD), F32)
            mixed = jnp.zeros((block_rows, HD), F32)
            for (maximum, total), ref in zip(pairs, in_refs):
                factor = jnp.exp2(maximum - joined)
                total_all = total_all + factor * total
                mixed = mixed + to_rows(factor, block_rows, 0) * ref[
                    k * block_rows : (k + 1) * block_rows, :
                ].astype(F32)
            merged.append((joined, total_all))
            for j in range(SLAB):
                out_refs[j][k * part : (k + 1) * part, :] = mixed[
                    j * part : (j + 1) * part
                ].astype(BF16)
        packed = pack_stats(merged).astype(BF16)
        for j in range(SLAB):
            out_refs[j][kvq * part :, :] = packed

    args = [blocks] if stacked else blocks
    return pl.pallas_call(
        kernel,
        out_shape=[pltpu.VMEM((out_rows, HD), BF16)] * SLAB,
        in_specs=[vmem_spec()] * len(args),
        out_specs=[vmem_spec()] * SLAB,
        name="merge",
    )(*near(args))


def finish(pieces, suffix_state, reward, cands, kvq, group):
    part = cands * group
    hq = kvq * group
    heads = SLAB * hq

    def kernel(*refs):
        piece_refs = refs[:SLAB]
        state_refs = refs[SLAB : SLAB + len(suffix_state)]
        reward_ref, out_ref, score_ref, scratch = refs[SLAB + len(suffix_state) :]
        split = suffix_state[0].shape[0] // heads
        mine = lax.axis_index("seq") % SLAB
        scores = [jnp.zeros((group, HD), F32) for _ in range(cands)]
        for j in range(SLAB):
            first = (mine ^ j) * hq
            piece = piece_refs[j][...].astype(F32)
            mix, stats = piece[: kvq * part], piece[kvq * part :]
            for k in range(kvq):
                maximum, total = unpack_stats(stats, k)
                maximum = to_rows(maximum, part, j * part)
                total = to_rows(total, part, j * part)
                weight = reward_ref[pl.ds(pl.multiple_of(first + k * group, 8), group), :]
                for r in range(cands):
                    base = r * heads if r < split else (r - split) * heads
                    max_ref, sum_ref, mix_ref = state_refs[:3] if r < split else state_refs[3:]
                    row = pl.ds(pl.multiple_of(r * heads + first + k * group, 8), group)
                    at = pl.ds(pl.multiple_of(base + first + k * group, 8), group)
                    cut = slice(r * group, (r + 1) * group)
                    home_max = max_ref[at, :]
                    here_max = jnp.broadcast_to(maximum[cut], (group, HD))
                    joined = jnp.maximum(home_max, here_max)
                    home = jnp.exp2(home_max - joined)
                    here = jnp.exp2(here_max - joined)
                    total_all = home * sum_ref[at, :] + here * total[cut]
                    mixed = home * mix_ref[at, :] + here * mix[k * part :][cut]
                    attended = (mixed / total_all).astype(BF16).astype(F32)
                    scratch[row, :] = attended
                    scores[r] = scores[r] + attended * weight
        for h in range(heads):
            out_ref[:, h * HD : (h + 1) * HD] = scratch[pl.ds(h, cands, stride=heads), :].astype(
                BF16
            )
        for r in range(cands):
            score_ref[r] = jnp.sum(scores[r])

    smem = pl.BlockSpec(memory_space=pltpu.SMEM)
    return pl.pallas_call(
        kernel,
        out_shape=[
            jax.ShapeDtypeStruct((cands, heads * HD), BF16),
            jax.ShapeDtypeStruct((cands,), F32),
        ],
        in_specs=[vmem_spec()] * (SLAB + len(suffix_state) + 1),
        out_specs=[vmem_spec(), smem],
        scratch_shapes=[pltpu.VMEM((cands * heads, HD), F32)],
        name="finish",
    )(*near(pieces), *near(suffix_state), *near([reward]))


def attend(queries, prompt_of, suffix_cache, suffix_blocks, prompt_cache, reward_weight):
    cands = queries.shape[0]
    heads = queries.shape[1] // HD
    kv_heads = prompt_cache.shape[2] // (2 * HD)
    group = heads // kv_heads
    kvq = kv_heads // SLAB
    devices = lax.axis_size("seq")
    outer = devices // SLAB

    def hop(x, step):
        return lax.ppermute(x, "seq", [(i, i ^ step) for i in range(devices)])

    def spread(arrays, step):
        return [arrays[0]] + [hop(arrays[i], step * i) for i in range(1, len(arrays))]

    def relay(own, near_part, far_part):
        far = hop(far_part, 2)
        return [own, hop(near_part, 1), far, hop(far, 1)]

    direct = is_direct(devices)
    columns = [[SLAB * z + i for z in range(outer)] for i in range(SLAB)]

    rows_q, live, q_parts, kv_parts = prepare(
        queries, prompt_of[:, 0], suffix_blocks, prompt_cache, kvq, group
    )
    far_kv = [hop(kv_parts[j], 2 + j) for j in range(2)]
    own, near_q, far_q, passed_q = relay(*q_parts)
    q_slab = pack(own, near_q, far_q, passed_q)
    early = (cands + 2) // 3
    *state, own_kv, near_kv = suffix_attend(
        0, early, live, rows_q, suffix_cache, kv_heads, prompt_cache
    )
    state += suffix_attend(early, cands - early, live, rows_q, suffix_cache, kv_heads)
    kv_parts = [own_kv, hop(near_kv, 1)] + far_kv
    if direct:
        q_all = spread([q_slab] * outer, SLAB)
    else:
        q_all = lax.all_gather(q_slab, "seq", axis_index_groups=columns)
    partial = prompt_attend(q_all, kv_parts, cands, kvq, group)
    if direct:
        partial = spread(partial, SLAB)
    else:
        partial = lax.all_to_all(
            partial, "seq", split_axis=0, concat_axis=0, axis_index_groups=columns, tiled=True
        )
    pieces = spread(merge(partial, cands, kvq, group), 1)
    reward = reward_weight.reshape(heads, HD)
    return tuple(finish(pieces, state, reward, cands, kvq, group))


def is_direct(devices):
    outer = devices // SLAB
    return outer == 4


def solution(mesh):
    placed = (
        P(("groups", "seq"), None),
        P(("groups", "seq"), None),
        P(("groups", "seq"), None, None),
        P(("groups", "seq")),
        P("groups", "seq", None),
        P(),
    )
    return jax.shard_map(
        attend,
        mesh=mesh,
        in_specs=placed,
        out_specs=(P(("groups", "seq"), None), P(("groups", "seq"))),
        check_vma=False,
    )
```

profile of v0, /device:TPU:0, one launch (start us, length us, event | category | flops | bytes accessed | tf_op | source)
XLA Modules:
  0.0 47.6 jit_solution(4198391666536080353)
XLA Ops:
  0.6 1.2 %prepare.1 = (bf16[192,128]{1,0:T(8,128)(2,1)S(1)}, s32[8,128]{1,0:T(8,128)S(1)}, bf16[56,128]{1,0:T(8,128)(2,1)S(1)}, bf16[56,128]{1,0:T(8,128)(2,1)S(1)}, bf16...) custom-call(bf16[3,8192]{1,0:T(4,128)(2,1)} %q_hbm.1, ...), custom_call_target="tpu_custom_call" | custom-call | tf_op jit(solution)/shard_map/prepare/pallas_call | solution.py:125
  1.8 0.0 copy-start
  1.9 2.2 %suffix.2 = (f32[64,128]{1,0:T(8,128)S(1)}, f32[64,128]{1,0:T(8,128)S(1)}, f32[64,128]{1,0:T(8,128)S(1)}, bf16[2,2,128,256]{3,2,1,0:T(8,128)(2,1)S(1)}, bf16[2,2,128,256]{3,2,1,0:T(8,128)(2,1)S(1)}) custom-call(s32[8,128]{1,0:T(8,128)S(1)} %get-tuple-element.28.live_ref, bf16[192,128]{1,0:T(8,128)(2,1)S(1)} %get-tuple-element.29.q_ref, ...), custom_call_target="tpu_custom_call" | custom-call | flops 134217728 | bytes 2097152 | tf_op jit(solution)/shard_map/suffix/pallas_call | solution.py:240
  4.1 0.6 %collective-permute-start.6 = (bf16[2,2,128,256]{3,2,1,0:T(8,128)(2,1)S(1)}, bf16[2,2,128,256]{3,2,1,0:T(8,128)(2,1)S(1)}, u32[]{:S(2)}, u32[]{:S(2)}) collective-permute-start(bf16[2,2,128,256]{3,2,1,0:T(8,128)(2,1)S(1)} %get-tuple-element.31), channel_id=1, source_target_pairs={{0,1},{1,0},{2,3},{3,2},{4,5},{5,4},{6,7},{7,6},{8,9},{9,8},{10,11... | collective-permute-start | bytes 786440 | tf_op jit(solution)/shard_map/ppermute | solution.py:467
  4.6 2.6 %collective-permute-start.7 = (bf16[2,2,128,256]{3,2,1,0:T(8,128)(2,1)S(1)}, bf16[2,2,128,256]{3,2,1,0:T(8,128)(2,1)S(1)}, u32[]{:S(2)}, u32[]{:S(2)}) collective-permute-start(bf16[2,2,128,256]{3,2,1,0:T(8,128)(2,1)S(1)} %get-tuple-element.32), channel_id=1, source_target_pairs={{0,2},{1,3},{2,0},{3,1},{4,6},{5,7},{6,4},{7,5},{8,10},{9,11},{10,... | collective-permute-start | bytes 786440 | tf_op jit(solution)/shard_map/ppermute | solution.py:467
  7.2 0.0 collective-permute-start.8
  7.2 1.7 %collective-permute-start.1 = (bf16[112,128]{1,0:T(8,128)(2,1)S(1)}, bf16[112,128]{1,0:T(8,128)(2,1)S(1)}, u32[]{:S(2)}, u32[]{:S(2)}) collective-permute-start(bf16[112,128]{1,0:T(8,128)(2,1)S(1)} %get-tuple-element.27), channel_id=1, source_target_pairs={{0,2},{1,3},{2,0},{3,1},{4,6},{5,7},{6,4},{7,5},{8,10},{9,11},{10,... | collective-permute-start | bytes 86024 | tf_op jit(solution)/shard_map/ppermute | solution.py:467
  9.0 11.3 %collective-permute-done.1.far_ref = bf16[112,128]{1,0:T(8,128)(2,1)S(1)} collective-permute-done((bf16[112,128]{1,0:T(8,128)(2,1)S(1)}, bf16[112,128]{1,0:T(8,128)(2,1)S(1)}, u32[]{:S(2)}, u32[]{:S(2)}) %collective-permute-start.1) | collective-permute-done | bytes 28704 | tf_op jit(solution)/shard_map/ppermute | solution.py:467
  20.3 0.0 collective-permute-start.2
  20.3 0.5 %collective-permute-start = (bf16[56,128]{1,0:T(8,128)(2,1)S(1)}, bf16[56,128]{1,0:T(8,128)(2,1)S(1)}, u32[]{:S(2)}, u32[]{:S(2)}) collective-permute-start(bf16[56,128]{1,0:T(8,128)(2,1)S(1)} %get-tuple-element.26), channel_id=1, source_target_pairs={{0,1},{1,0},{2,3},{3,2},{4,5},{5,4},{6,7},{7,6},{8,9},{9,8},{10,11... | collective-permute-start | bytes 43016 | tf_op jit(solution)/shard_map/ppermute | solution.py:467
  20.8 0.8 %collective-permute-done.near_ref = bf16[56,128]{1,0:T(8,128)(2,1)S(1)} collective-permute-done((bf16[56,128]{1,0:T(8,128)(2,1)S(1)}, bf16[56,128]{1,0:T(8,128)(2,1)S(1)}, u32[]{:S(2)}, u32[]{:S(2)}) %collective-permute-start) | collective-permute-done | bytes 14368 | tf_op jit(solution)/shard_map/ppermute | solution.py:467
  21.7 0.0 collective-permute-done.2.passed_ref
  21.7 1.9 %collective-permute-start.3 = (bf16[200,128]{1,0:T(8,128)(2,1)S(1)}, bf16[200,128]{1,0:T(8,128)(2,1)S(1)}, u32[]{:S(2)}, u32[]{:S(2)}) collective-permute-start(bf16[200,128]{1,0:T(8,128)(2,1)S(1)} %pack.1.refs_0_), channel_id=1, source_target_pairs={{0,4},{1,5},{2,6},{3,7},{4,0},{5,1},{6,2},{7,3},{8,12},{9,13},{10,... | collective-permute-start | bytes 153608 | tf_op jit(solution)/shard_map/ppermute | solution.py:467
  23.6 2.6 %collective-permute-start.4 = (bf16[200,128]{1,0:T(8,128)(2,1)S(1)}, bf16[200,128]{1,0:T(8,128)(2,1)S(1)}, u32[]{:S(2)}, u32[]{:S(2)}) collective-permute-start(bf16[200,128]{1,0:T(8,128)(2,1)S(1)} %pack.1.refs_0_), channel_id=1, source_target_pairs={{0,8},{1,9},{2,10},{3,11},{4,12},{5,13},{6,14},{7,15},{8,0},{9,1},... | collective-permute-start | bytes 153608 | tf_op jit(solution)/shard_map/ppermute | solution.py:467
  26.2 0.0 collective-permute-done.3.refs_1_
  26.2 4.1 %collective-permute-start.5 = (bf16[200,128]{1,0:T(8,128)(2,1)S(1)}, bf16[200,128]{1,0:T(8,128)(2,1)S(1)}, u32[]{:S(2)}, u32[]{:S(2)}) collective-permute-start(bf16[200,128]{1,0:T(8,128)(2,1)S(1)} %pack.1.refs_0_), channel_id=1, source_target_pairs={{0,12},{1,13},{2,14},{3,15},{4,8},{5,9},{6,10},{7,11},{8,4},{9,5},... | collective-permute-start | bytes 153608 | tf_op jit(solution)/shard_map/ppermute | solution.py:467
  30.2 0.0 collective-permute-done.4.refs_2_
  30.3 2.1 %collective-permute-done.5.refs_3_ = bf16[200,128]{1,0:T(8,128)(2,1)S(1)} collective-permute-done((bf16[200,128]{1,0:T(8,128)(2,1)S(1)}, bf16[200,128]{1,0:T(8,128)(2,1)S(1)}, u32[]{:S(2)}, u32[]{:S(2)}) %collective-permute-start.5) | collective-permute-done | bytes 51232 | tf_op jit(solution)/shard_map/ppermute | solution.py:467
  32.3 0.0 collective-permute-done.6.refs_5_
  32.3 0.0 collective-permute-done.7.refs_6_
  32.3 0.0 collective-permute-done.8.refs_7_
  32.3 1.0 %prompt.1 = (bf16[200,128]{1,0:T(8,128)(2,1)S(1)}, bf16[200,128]{1,0:T(8,128)(2,1)S(1)}, bf16[200,128]{1,0:T(8,128)(2,1)S(1)}, bf16[200,128]{1,0:T(8,128)(2,1)S(1)}) custom-call(bf16[200,128]{1,0:T(8,128)(2,1)S(1)} %pack.1.refs_0_, bf16[200,128]{1,0:T(8,128)(2,1)S(1)} %collective-permute-done.3.refs_1_, bf16[200,128]{1,0:T(8,128)(2,1)S(1)} %collective-permute-done.4.refs_2_, ...), custom_call_target="tpu_custom_call" | custom-call | tf_op jit(solution)/shard_map/prompt/pallas_call | solution.py:342
  33.4 1.2 %collective-permute-start.10 = (bf16[200,128]{1,0:T(8,128)(2,1)S(1)}, bf16[200,128]{1,0:T(8,128)(2,1)S(1)}, u32[]{:S(2)}, u32[]{:S(2)}) collective-permute-start(bf16[200,128]{1,0:T(8,128)(2,1)S(1)} %get-tuple-element.36), channel_id=1, source_target_pairs={{0,8},{1,9},{2,10},{3,11},{4,12},{5,13},{6,14},{7,15},{8,0},{9,1},... | collective-permute-start | bytes 153608 | tf_op jit(solution)/shard_map/ppermute | solution.py:467
  34.6 2.8 %collective-permute-start.11 = (bf16[200,128]{1,0:T(8,128)(2,1)S(1)}, bf16[200,128]{1,0:T(8,128)(2,1)S(1)}, u32[]{:S(2)}, u32[]{:S(2)}) collective-permute-start(bf16[200,128]{1,0:T(8,128)(2,1)S(1)} %get-tuple-element.37), channel_id=1, source_target_pairs={{0,12},{1,13},{2,14},{3,15},{4,8},{5,9},{6,10},{7,11},{8,4},{9,5},... | collective-permute-start | bytes 153608 | tf_op jit(solution)/shard_map/ppermute | solution.py:467
  37.3 0.5 %collective-permute-start.9 = (bf16[200,128]{1,0:T(8,128)(2,1)S(1)}, bf16[200,128]{1,0:T(8,128)(2,1)S(1)}, u32[]{:S(2)}, u32[]{:S(2)}) collective-permute-start(bf16[200,128]{1,0:T(8,128)(2,1)S(1)} %get-tuple-element.35), channel_id=1, source_target_pairs={{0,4},{1,5},{2,6},{3,7},{4,0},{5,1},{6,2},{7,3},{8,12},{9,13},{10,... | collective-permute-start | bytes 153608 | tf_op jit(solution)/shard_map/ppermute | solution.py:467
  37.8 0.7 %collective-permute-done.10.refs_2_ = bf16[200,128]{1,0:T(8,128)(2,1)S(1)} collective-permute-done((bf16[200,128]{1,0:T(8,128)(2,1)S(1)}, bf16[200,128]{1,0:T(8,128)(2,1)S(1)}, u32[]{:S(2)}, u32[]{:S(2)}) %collective-permute-start.10) | collective-permute-done | bytes 51232 | tf_op jit(solution)/shard_map/ppermute | solution.py:467
  38.5 2.0 %collective-permute-done.11.refs_3_ = bf16[200,128]{1,0:T(8,128)(2,1)S(1)} collective-permute-done((bf16[200,128]{1,0:T(8,128)(2,1)S(1)}, bf16[200,128]{1,0:T(8,128)(2,1)S(1)}, u32[]{:S(2)}, u32[]{:S(2)}) %collective-permute-start.11) | collective-permute-done | bytes 51232 | tf_op jit(solution)/shard_map/ppermute | solution.py:467
  40.5 1.0 %collective-permute-done.9.refs_1_ = bf16[200,128]{1,0:T(8,128)(2,1)S(1)} collective-permute-done((bf16[200,128]{1,0:T(8,128)(2,1)S(1)}, bf16[200,128]{1,0:T(8,128)(2,1)S(1)}, u32[]{:S(2)}, u32[]{:S(2)}) %collective-permute-start.9) | collective-permute-done | bytes 51232 | tf_op jit(solution)/shard_map/ppermute | solution.py:467
  41.4 0.2 merge.1
  41.6 0.1 collective-permute-start.12
  41.7 1.2 %collective-permute-start.13 = (bf16[56,128]{1,0:T(8,128)(2,1)S(1)}, bf16[56,128]{1,0:T(8,128)(2,1)S(1)}, u32[]{:S(2)}, u32[]{:S(2)}) collective-permute-start(bf16[56,128]{1,0:T(8,128)(2,1)S(1)} %get-tuple-element.40), channel_id=1, source_target_pairs={{0,2},{1,3},{2,0},{3,1},{4,6},{5,7},{6,4},{7,5},{8,10},{9,11},{10,... | collective-permute-start | bytes 43016 | tf_op jit(solution)/shard_map/ppermute | solution.py:467
  42.9 0.7 %collective-permute-start.14 = (bf16[56,128]{1,0:T(8,128)(2,1)S(1)}, bf16[56,128]{1,0:T(8,128)(2,1)S(1)}, u32[]{:S(2)}, u32[]{:S(2)}) collective-permute-start(bf16[56,128]{1,0:T(8,128)(2,1)S(1)} %get-tuple-element.41), channel_id=1, source_target_pairs={{0,3},{1,2},{2,1},{3,0},{4,7},{5,6},{6,5},{7,4},{8,11},{9,10},{10,... | collective-permute-start | bytes 43016 | tf_op jit(solution)/shard_map/ppermute | solution.py:467
  43.6 3.1 %suffix.3 = (f32[128,128]{1,0:T(8,128)S(1)}, f32[128,128]{1,0:T(8,128)S(1)}, f32[128,128]{1,0:T(8,128)S(1)}) custom-call(s32[8,128]{1,0:T(8,128)S(1)} %get-tuple-element.28.live_ref, bf16[192,128]{1,0:T(8,128)(2,1)S(1)} %get-tuple-element.29.q_ref, bf16[3,512,2048]{2,1,0:T(8,128)(2,1)} %cache_ref.5), custom_call_target="tpu_custom_call" | custom-call | flops 268435456 | bytes 4194304 | tf_op jit(solution)/shard_map/suffix/pallas_call | solution.py:240
  46.6 0.0 collective-permute-done.12.refs_1_
  46.7 0.0 collective-permute-done.13.refs_2_
  46.7 0.0 collective-permute-done.14.refs_3_
  46.7 0.0 copy-done
  46.7 0.9 %finish.1 = (bf16[3,8192]{1,0:T(4,128)(2,1)}, f32[3]{0:T(128)}) custom-call(bf16[56,128]{1,0:T(8,128)(2,1)S(1)} %get-tuple-element.38.refs_0_, bf16[56,128]{1,0:T(8,128)(2,1)S(1)} %collective-permute-done.12.refs_1_, bf16[56,128]{1,0:T(8,128)(2,1)S(1)} %collective-permute-done.13.refs_2_, bf16[56,128]{1,0:T(8,128)(2,1)S(1)} %collective-permute-done.14.refs_3_, ...), custom_call_target="tpu_custom_call" | custom-call | tf_op jit(solution)/shard_map/finish/pallas_call | solution.py:444
  (1 shorter events, 0.0 us)
Async XLA Ops:
  1.8 44.8 %copy-start = (f32[8192]{0:T(1024)S(1)}, f32[8192]{0:T(1024)}, u32[]{:S(2)}) copy-start(f32[8192]{0:T(1024)} %param.11) | copy-start | bytes 98308
  4.1 28.3 %collective-permute-start.6 = (bf16[2,2,128,256]{3,2,1,0:T(8,128)(2,1)S(1)}, bf16[2,2,128,256]{3,2,1,0:T(8,128)(2,1)S(1)}, u32[]{:S(2)}, u32[]{:S(2)}) collective-permute-start(bf16[2,2,128,256]{3,2,1,0:T(8,128)(2,1)S(1)} %get-tuple-element.31), channel_id=1, source_target_pairs={{0,1},{1,0},{2,3},{3,2},{4,5},{5,4},{6,7},{7,6},{8,9},{9,8},{10,11... | collective-permute-start | bytes 786440 | tf_op jit(solution)/shard_map/ppermute | solution.py:467
  4.6 27.7 %collective-permute-start.7 = (bf16[2,2,128,256]{3,2,1,0:T(8,128)(2,1)S(1)}, bf16[2,2,128,256]{3,2,1,0:T(8,128)(2,1)S(1)}, u32[]{:S(2)}, u32[]{:S(2)}) collective-permute-start(bf16[2,2,128,256]{3,2,1,0:T(8,128)(2,1)S(1)} %get-tuple-element.32), channel_id=1, source_target_pairs={{0,2},{1,3},{2,0},{3,1},{4,6},{5,7},{6,4},{7,5},{8,10},{9,11},{10,... | collective-permute-start | bytes 786440 | tf_op jit(solution)/shard_map/ppermute | solution.py:467
  7.2 25.1 %collective-permute-start.8 = (bf16[2,2,128,256]{3,2,1,0:T(8,128)(2,1)S(1)}, bf16[2,2,128,256]{3,2,1,0:T(8,128)(2,1)S(1)}, u32[]{:S(2)}, u32[]{:S(2)}) collective-permute-start(bf16[2,2,128,256]{3,2,1,0:T(8,128)(2,1)S(1)} %get-tuple-element.33), channel_id=1, source_target_pairs={{0,3},{1,2},{2,1},{3,0},{4,7},{5,6},{6,5},{7,4},{8,11},{9,10},{10,... | collective-permute-start | bytes 786440 | tf_op jit(solution)/shard_map/ppermute | solution.py:467
  7.2 13.1 %collective-permute-start.1 = (bf16[112,128]{1,0:T(8,128)(2,1)S(1)}, bf16[112,128]{1,0:T(8,128)(2,1)S(1)}, u32[]{:S(2)}, u32[]{:S(2)}) collective-permute-start(bf16[112,128]{1,0:T(8,128)(2,1)S(1)} %get-tuple-element.27), channel_id=1, source_target_pairs={{0,2},{1,3},{2,0},{3,1},{4,6},{5,7},{6,4},{7,5},{8,10},{9,11},{10,... | collective-permute-start | bytes 86024 | tf_op jit(solution)/shard_map/ppermute | solution.py:467
  20.3 1.4 %collective-permute-start.2 = (bf16[112,128]{1,0:T(8,128)(2,1)S(1)}, bf16[112,128]{1,0:T(8,128)(2,1)S(1)}, u32[]{:S(2)}, u32[]{:S(2)}) collective-permute-start(bf16[112,128]{1,0:T(8,128)(2,1)S(1)} %collective-permute-done.1.far_ref), channel_id=1, source_target_pairs={{0,1},{1,0},{2,3},{3,2},{4,5},{5,4},{6,7},{7,6},{8,9},{9,8},{10,11... | collective-permute-start | bytes 86024 | tf_op jit(solution)/shard_map/ppermute | solution.py:467
  20.3 1.3 %collective-permute-start = (bf16[56,128]{1,0:T(8,128)(2,1)S(1)}, bf16[56,128]{1,0:T(8,128)(2,1)S(1)}, u32[]{:S(2)}, u32[]{:S(2)}) collective-permute-start(bf16[56,128]{1,0:T(8,128)(2,1)S(1)} %get-tuple-element.26), channel_id=1, source_target_pairs={{0,1},{1,0},{2,3},{3,2},{4,5},{5,4},{6,7},{7,6},{8,9},{9,8},{10,11... | collective-permute-start | bytes 43016 | tf_op jit(solution)/shard_map/ppermute | solution.py:467
  21.7 4.5 %collective-permute-start.3 = (bf16[200,128]{1,0:T(8,128)(2,1)S(1)}, bf16[200,128]{1,0:T(8,128)(2,1)S(1)}, u32[]{:S(2)}, u32[]{:S(2)}) collective-permute-start(bf16[200,128]{1,0:T(8,128)(2,1)S(1)} %pack.1.refs_0_), channel_id=1, source_target_pairs={{0,4},{1,5},{2,6},{3,7},{4,0},{5,1},{6,2},{7,3},{8,12},{9,13},{10,... | collective-permute-start | bytes 153608 | tf_op jit(solution)/shard_map/ppermute | solution.py:467
  23.6 6.7 %collective-permute-start.4 = (bf16[200,128]{1,0:T(8,128)(2,1)S(1)}, bf16[200,128]{1,0:T(8,128)(2,1)S(1)}, u32[]{:S(2)}, u32[]{:S(2)}) collective-permute-start(bf16[200,128]{1,0:T(8,128)(2,1)S(1)} %pack.1.refs_0_), channel_id=1, source_target_pairs={{0,8},{1,9},{2,10},{3,11},{4,12},{5,13},{6,14},{7,15},{8,0},{9,1},... | collective-permute-start | bytes 153608 | tf_op jit(solution)/shard_map/ppermute | solution.py:467
  26.2 6.2 %collective-permute-start.5 = (bf16[200,128]{1,0:T(8,128)(2,1)S(1)}, bf16[200,128]{1,0:T(8,128)(2,1)S(1)}, u32[]{:S(2)}, u32[]{:S(2)}) collective-permute-start(bf16[200,128]{1,0:T(8,128)(2,1)S(1)} %pack.1.refs_0_), channel_id=1, source_target_pairs={{0,12},{1,13},{2,14},{3,15},{4,8},{5,9},{6,10},{7,11},{8,4},{9,5},... | collective-permute-start | bytes 153608 | tf_op jit(solution)/shard_map/ppermute | solution.py:467
  33.4 5.1 %collective-permute-start.10 = (bf16[200,128]{1,0:T(8,128)(2,1)S(1)}, bf16[200,128]{1,0:T(8,128)(2,1)S(1)}, u32[]{:S(2)}, u32[]{:S(2)}) collective-permute-start(bf16[200,128]{1,0:T(8,128)(2,1)S(1)} %get-tuple-element.36), channel_id=1, source_target_pairs={{0,8},{1,9},{2,10},{3,11},{4,12},{5,13},{6,14},{7,15},{8,0},{9,1},... | collective-permute-start | bytes 153608 | tf_op jit(solution)/shard_map/ppermute | solution.py:467
  34.6 5.9 %collective-permute-start.11 = (bf16[200,128]{1,0:T(8,128)(2,1)S(1)}, bf16[200,128]{1,0:T(8,128)(2,1)S(1)}, u32[]{:S(2)}, u32[]{:S(2)}) collective-permute-start(bf16[200,128]{1,0:T(8,128)(2,1)S(1)} %get-tuple-element.37), channel_id=1, source_target_pairs={{0,12},{1,13},{2,14},{3,15},{4,8},{5,9},{6,10},{7,11},{8,4},{9,5},... | collective-permute-start | bytes 153608 | tf_op jit(solution)/shard_map/ppermute | solution.py:467
  37.3 4.1 %collective-permute-start.9 = (bf16[200,128]{1,0:T(8,128)(2,1)S(1)}, bf16[200,128]{1,0:T(8,128)(2,1)S(1)}, u32[]{:S(2)}, u32[]{:S(2)}) collective-permute-start(bf16[200,128]{1,0:T(8,128)(2,1)S(1)} %get-tuple-element.35), channel_id=1, source_target_pairs={{0,4},{1,5},{2,6},{3,7},{4,0},{5,1},{6,2},{7,3},{8,12},{9,13},{10,... | collective-permute-start | bytes 153608 | tf_op jit(solution)/shard_map/ppermute | solution.py:467
  41.6 5.0 %collective-permute-start.12 = (bf16[56,128]{1,0:T(8,128)(2,1)S(1)}, bf16[56,128]{1,0:T(8,128)(2,1)S(1)}, u32[]{:S(2)}, u32[]{:S(2)}) collective-permute-start(bf16[56,128]{1,0:T(8,128)(2,1)S(1)} %get-tuple-element.39), channel_id=1, source_target_pairs={{0,1},{1,0},{2,3},{3,2},{4,5},{5,4},{6,7},{7,6},{8,9},{9,8},{10,11... | collective-permute-start | bytes 43016 | tf_op jit(solution)/shard_map/ppermute | solution.py:467
  41.7 4.9 %collective-permute-start.13 = (bf16[56,128]{1,0:T(8,128)(2,1)S(1)}, bf16[56,128]{1,0:T(8,128)(2,1)S(1)}, u32[]{:S(2)}, u32[]{:S(2)}) collective-permute-start(bf16[56,128]{1,0:T(8,128)(2,1)S(1)} %get-tuple-element.40), channel_id=1, source_target_pairs={{0,2},{1,3},{2,0},{3,1},{4,6},{5,7},{6,4},{7,5},{8,10},{9,11},{10,... | collective-permute-start | bytes 43016 | tf_op jit(solution)/shard_map/ppermute | solution.py:467
  42.9 3.8 %collective-permute-start.14 = (bf16[56,128]{1,0:T(8,128)(2,1)S(1)}, bf16[56,128]{1,0:T(8,128)(2,1)S(1)}, u32[]{:S(2)}, u32[]{:S(2)}) collective-permute-start(bf16[56,128]{1,0:T(8,128)(2,1)S(1)} %get-tuple-element.41), channel_id=1, source_target_pairs={{0,3},{1,2},{2,1},{3,0},{4,7},{5,6},{6,5},{7,4},{8,11},{9,10},{10,... | collective-permute-start | bytes 43016 | tf_op jit(solution)/shard_map/ppermute | solution.py:467
where the time goes:
time: 47.7 us; the launch traced here: 47.6 us
  starting transfers between devices  20.3 us (43%)
  waiting for transfers between devices  17.9 us (38%)
  Pallas kernels  8.54 us (18%)
  between operations  0.74 us (2%)
    ppermute x15, starting transfers between devices, hop(): return lax.ppermute(x, 'seq', [(i, i ^ step) for i in range(devices)])  20.3 us
    ppermute x15, waiting for transfers between devices, hop(): return lax.ppermute(x, 'seq', [(i, i ^ step) for i in range(devices)])  17.9 us
    pallas_call x2, Pallas kernels, suffix_attend(): pl.pallas_call(kernel, out_shape=[pltpu.VMEM((count * heads, HD), F32)] *...  5.27 us
    pallas_call x1, Pallas kernels, prepare(): pl.pallas_call(kernel, out_shape=[pltpu.VMEM((cands * heads, HD), BF16),...  1.2 us
    pallas_call x1, Pallas kernels, prompt_attend(): pl.pallas_call(kernel, out_shape=[pltpu.VMEM((out_rows, HD), BF16)] * out...  1 us
  transfers between devices with their start and end apart: 15, of which 6 were waited for; matrix products, arithmetic and copies ran while one was open for 0% of the time, Pallas kernels for 6%

commit v1 on v0

--- a/solution.py
+++ b/solution.py
@@ -10,7 +10,6 @@
 
 HD = 128
 BLOCK = 128
-LOG2E = 1.4426950408889634
 
 SLAB = 4
 F32 = jnp.float32
@@ -81,6 +80,12 @@
         kv_out = rest[5:7]
         q_ref, ids_ref, blocks_ref, scratch, sem, kv_sem = rest[7:]
         mine = lax.axis_index("seq") % SLAB
+        q_copy = pltpu.make_async_copy(q_hbm, q_ref, sem.at[0])
+        q_copy.start()
+        ids_copy = pltpu.make_async_copy(ids_hbm, ids_ref, sem.at[1])
+        ids_copy.start()
+        blocks_copy = pltpu.make_async_copy(blocks_hbm, blocks_ref, sem.at[2])
+        blocks_copy.start()
         copies = []
         for j in range(2):
             for side in range(2):
@@ -90,12 +95,6 @@
                 )
                 copy.start()
                 copies.append(copy)
-        q_copy = pltpu.make_async_copy(q_hbm, q_ref, sem.at[0])
-        q_copy.start()
-        ids_copy = pltpu.make_async_copy(ids_hbm, ids_ref, sem.at[1])
-        ids_copy.start()
-        blocks_copy = pltpu.make_async_copy(blocks_hbm, blocks_ref, sem.at[2])
-        blocks_copy.start()
         q_copy.wait()
         for h in range(heads):
             scratch[pl.ds(h, cands, stride=heads), :] = q_ref[:, h * HD : (h + 1) * HD].astype(F32)
@@ -216,12 +215,12 @@
             fetches[2 * c].wait()
             logits = lax.dot_general(
                 wide, keys[c], (((1,), (1,)), ((), ())), preferred_element_type=F32
-            ) * (LOG2E * HD ** (-0.5))
+            ) * HD ** (-0.5)
             live_row = jnp.concatenate([live_ref[first + c : first + c + 1, :]] * (length // HD), axis=1)
             live = position < live_row
             logits = jnp.where(live, logits, floor_logit)
             maxima = jnp.max(logits, axis=1, keepdims=True)
-            exponent = jnp.where(live, jnp.exp2(logits - maxima), 0.0)
+            exponent = jnp.where(live, jnp.exp(logits - maxima), 0.0)
             totals = jnp.sum(exponent, axis=1, keepdims=True)
             fetches[2 * c + 1].wait()
             mixed = jnp.dot(exponent.astype(BF16), values[c], preferred_element_type=F32)
@@ -312,9 +311,9 @@
 
             logits = lax.dot_general(
                 q, both(0), (((1,), (1,)), ((), ())), preferred_element_type=F32
-            ) * (LOG2E * HD ** (-0.5))
+            ) * HD ** (-0.5)
             maxima = jnp.max(logits, axis=1, keepdims=True).astype(BF16).astype(F32)
-            exponent = jnp.exp2(logits - maxima)
+            exponent = jnp.exp(logits - maxima)
             totals = jnp.sum(exponent, axis=1, keepdims=True)
             wide = jnp.dot(exponent.astype(BF16), both(1), preferred_element_type=F32)
             mixed = wide[:, :HD]
@@ -372,7 +371,7 @@
             total_all = jnp.zeros((1, HD), F32)
             mixed = jnp.zeros((block_rows, HD), F32)
             for (maximum, total), ref in zip(pairs, in_refs):
-                factor = jnp.exp2(maximum - joined)
+                factor = jnp.exp(maximum - joined)
                 total_all = total_all + factor * total
                 mixed = mixed + to_rows(factor, block_rows, 0) * ref[
                     k * block_rows : (k + 1) * block_rows, :
@@ -426,8 +425,8 @@
                     home_max = max_ref[at, :]
                     here_max = jnp.broadcast_to(maximum[cut], (group, HD))
                     joined = jnp.maximum(home_max, here_max)
-                    home = jnp.exp2(home_max - joined)
-                    here = jnp.exp2(here_max - joined)
+                    home = jnp.exp(home_max - joined)
+                    here = jnp.exp(here_max - joined)
                     total_all = home * sum_ref[at, :] + here * total[cut]
                     mixed = home * mix_ref[at, :] + here * mix[k * part :][cut]
                     attended = (mixed / total_all).astype(BF16).astype(F32)

time: 47.7 us -> 47.8 us (level)
  transfers between devices with their start and end apart: 15 -> 15, of which waited for: 6 -> 6; matrix products, arithmetic and copies ran while one was open for 0% -> 0% of each run, Pallas kernels for 6% -> 7%
where the time goes in v1:
time: 47.8 us; the launch traced here: 47.6 us
  starting transfers between devices  20.4 us (43%)
  waiting for transfers between devices  17.9 us (37%)
  Pallas kernels  8.59 us (18%)
  between operations  0.74 us (2%)
    ppermute x15, starting transfers between devices, hop(): return lax.ppermute(x, 'seq', [(i, i ^ step) for i in range(devices)])  20.4 us
    ppermute x15, waiting for transfers between devices, hop(): return lax.ppermute(x, 'seq', [(i, i ^ step) for i in range(devices)])  17.9 us
    pallas_call x2, Pallas kernels, suffix_attend(): pl.pallas_call(kernel, out_shape=[pltpu.VMEM((count * heads, HD), F32)] *...  5.28 us
    pallas_call x1, Pallas kernels, prepare(): pl.pallas_call(kernel, out_shape=[pltpu.VMEM((cands * heads, HD), BF16),...  1.2 us
    pallas_call x1, Pallas kernels, prompt_attend(): pl.pallas_call(kernel, out_shape=[pltpu.VMEM((out_rows, HD), BF16)] * out...  1.03 us
  transfers between devices with their start and end apart: 15, of which 6 were waited for; matrix products, arithmetic and copies ran while one was open for 0% of the time, Pallas kernels for 7%

profile of v1, /device:TPU:0, one launch (start us, length us, event | category | flops | bytes accessed | tf_op | source)
XLA Modules:
  0.0 47.6 jit_solution(13349626548690990863)
XLA Ops:
  0.6 1.2 %prepare.1 = (bf16[192,128]{1,0:T(8,128)(2,1)S(1)}, s32[8,128]{1,0:T(8,128)S(1)}, bf16[56,128]{1,0:T(8,128)(2,1)S(1)}, bf16[56,128]{1,0:T(8,128)(2,1)S(1)}, bf16...) custom-call(bf16[3,8192]{1,0:T(4,128)(2,1)} %q_hbm.1, ...), custom_call_target="tpu_custom_call" | custom-call | tf_op jit(solution)/shard_map/prepare/pallas_call | solution.py:124
  1.8 0.0 copy-start
  1.9 2.2 %suffix.2 = (f32[64,128]{1,0:T(8,128)S(1)}, f32[64,128]{1,0:T(8,128)S(1)}, f32[64,128]{1,0:T(8,128)S(1)}, bf16[2,2,128,256]{3,2,1,0:T(8,128)(2,1)S(1)}, bf16[2,2,128,256]{3,2,1,0:T(8,128)(2,1)S(1)}) custom-call(s32[8,128]{1,0:T(8,128)S(1)} %get-tuple-element.28.live_ref, bf16[192,128]{1,0:T(8,128)(2,1)S(1)} %get-tuple-element.29.q_ref, ...), custom_call_target="tpu_custom_call" | custom-call | flops 134217728 | bytes 2097152 | tf_op jit(solution)/shard_map/suffix/pallas_call | solution.py:239
  4.1 0.6 %collective-permute-start.6 = (bf16[2,2,128,256]{3,2,1,0:T(8,128)(2,1)S(1)}, bf16[2,2,128,256]{3,2,1,0:T(8,128)(2,1)S(1)}, u32[]{:S(2)}, u32[]{:S(2)}) collective-permute-start(bf16[2,2,128,256]{3,2,1,0:T(8,128)(2,1)S(1)} %get-tuple-element.31), channel_id=1, source_target_pairs={{0,1},{1,0},{2,3},{3,2},{4,5},{5,4},{6,7},{7,6},{8,9},{9,8},{10,11... | collective-permute-start | bytes 786440 | tf_op jit(solution)/shard_map/ppermute | solution.py:466
  4.6 2.6 %collective-permute-start.7 = (bf16[2,2,128,256]{3,2,1,0:T(8,128)(2,1)S(1)}, bf16[2,2,128,256]{3,2,1,0:T(8,128)(2,1)S(1)}, u32[]{:S(2)}, u32[]{:S(2)}) collective-permute-start(bf16[2,2,128,256]{3,2,1,0:T(8,128)(2,1)S(1)} %get-tuple-element.32), channel_id=1, source_target_pairs={{0,2},{1,3},{2,0},{3,1},{4,6},{5,7},{6,4},{7,5},{8,10},{9,11},{10,... | collective-permute-start | bytes 786440 | tf_op jit(solution)/shard_map/ppermute | solution.py:466
  7.2 0.0 collective-permute-start.8
  7.2 1.7 %collective-permute-start.1 = (bf16[112,128]{1,0:T(8,128)(2,1)S(1)}, bf16[112,128]{1,0:T(8,128)(2,1)S(1)}, u32[]{:S(2)}, u32[]{:S(2)}) collective-permute-start(bf16[112,128]{1,0:T(8,128)(2,1)S(1)} %get-tuple-element.27), channel_id=1, source_target_pairs={{0,2},{1,3},{2,0},{3,1},{4,6},{5,7},{6,4},{7,5},{8,10},{9,11},{10,... | collective-permute-start | bytes 86024 | tf_op jit(solution)/shard_map/ppermute | solution.py:466
  9.0 11.3 %collective-permute-done.1.far_ref = bf16[112,128]{1,0:T(8,128)(2,1)S(1)} collective-permute-done((bf16[112,128]{1,0:T(8,128)(2,1)S(1)}, bf16[112,128]{1,0:T(8,128)(2,1)S(1)}, u32[]{:S(2)}, u32[]{:S(2)}) %collective-permute-start.1) | collective-permute-done | bytes 28704 | tf_op jit(solution)/shard_map/ppermute | solution.py:466
  20.3 0.0 collective-permute-start.2
  20.3 0.5 %collective-permute-start = (bf16[56,128]{1,0:T(8,128)(2,1)S(1)}, bf16[56,128]{1,0:T(8,128)(2,1)S(1)}, u32[]{:S(2)}, u32[]{:S(2)}) collective-permute-start(bf16[56,128]{1,0:T(8,128)(2,1)S(1)} %get-tuple-element.26), channel_id=1, source_target_pairs={{0,1},{1,0},{2,3},{3,2},{4,5},{5,4},{6,7},{7,6},{8,9},{9,8},{10,11... | collective-permute-start | bytes 43016 | tf_op jit(solution)/shard_map/ppermute | solution.py:466
  20.8 0.8 %collective-permute-done.near_ref = bf16[56,128]{1,0:T(8,128)(2,1)S(1)} collective-permute-done((bf16[56,128]{1,0:T(8,128)(2,1)S(1)}, bf16[56,128]{1,0:T(8,128)(2,1)S(1)}, u32[]{:S(2)}, u32[]{:S(2)}) %collective-permute-start) | collective-permute-done | bytes 14368 | tf_op jit(solution)/shard_map/ppermute | solution.py:466
  21.7 0.0 collective-permute-done.2.passed_ref
  21.7 1.9 %collective-permute-start.3 = (bf16[200,128]{1,0:T(8,128)(2,1)S(1)}, bf16[200,128]{1,0:T(8,128)(2,1)S(1)}, u32[]{:S(2)}, u32[]{:S(2)}) collective-permute-start(bf16[200,128]{1,0:T(8,128)(2,1)S(1)} %pack.1.refs_0_), channel_id=1, source_target_pairs={{0,4},{1,5},{2,6},{3,7},{4,0},{5,1},{6,2},{7,3},{8,12},{9,13},{10,... | collective-permute-start | bytes 153608 | tf_op jit(solution)/shard_map/ppermute | solution.py:466
  23.6 2.6 %collective-permute-start.4 = (bf16[200,128]{1,0:T(8,128)(2,1)S(1)}, bf16[200,128]{1,0:T(8,128)(2,1)S(1)}, u32[]{:S(2)}, u32[]{:S(2)}) collective-permute-start(bf16[200,128]{1,0:T(8,128)(2,1)S(1)} %pack.1.refs_0_), channel_id=1, source_target_pairs={{0,8},{1,9},{2,10},{3,11},{4,12},{5,13},{6,14},{7,15},{8,0},{9,1},... | collective-permute-start | bytes 153608 | tf_op jit(solution)/shard_map/ppermute | solution.py:466
  26.2 0.0 collective-permute-done.3.refs_1_
  26.2 4.1 %collective-permute-start.5 = (bf16[200,128]{1,0:T(8,128)(2,1)S(1)}, bf16[200,128]{1,0:T(8,128)(2,1)S(1)}, u32[]{:S(2)}, u32[]{:S(2)}) collective-permute-start(bf16[200,128]{1,0:T(8,128)(2,1)S(1)} %pack.1.refs_0_), channel_id=1, source_target_pairs={{0,12},{1,13},{2,14},{3,15},{4,8},{5,9},{6,10},{7,11},{8,4},{9,5},... | collective-permute-start | bytes 153608 | tf_op jit(solution)/shard_map/ppermute | solution.py:466
  30.2 0.0 collective-permute-done.4.refs_2_
  30.3 2.1 %collective-permute-done.5.refs_3_ = bf16[200,128]{1,0:T(8,128)(2,1)S(1)} collective-permute-done((bf16[200,128]{1,0:T(8,128)(2,1)S(1)}, bf16[200,128]{1,0:T(8,128)(2,1)S(1)}, u32[]{:S(2)}, u32[]{:S(2)}) %collective-permute-start.5) | collective-permute-done | bytes 51232 | tf_op jit(solution)/shard_map/ppermute | solution.py:466
  32.3 0.0 collective-permute-done.6.refs_5_
  32.3 0.0 collective-permute-done.7.refs_6_
  32.3 0.0 collective-permute-done.8.refs_7_
  32.4 1.0 %prompt.1 = (bf16[200,128]{1,0:T(8,128)(2,1)S(1)}, bf16[200,128]{1,0:T(8,128)(2,1)S(1)}, bf16[200,128]{1,0:T(8,128)(2,1)S(1)}, bf16[200,128]{1,0:T(8,128)(2,1)S(1)}) custom-call(bf16[200,128]{1,0:T(8,128)(2,1)S(1)} %pack.1.refs_0_, bf16[200,128]{1,0:T(8,128)(2,1)S(1)} %collective-permute-done.3.refs_1_, bf16[200,128]{1,0:T(8,128)(2,1)S(1)} %collective-permute-done.4.refs_2_, ...), custom_call_target="tpu_custom_call" | custom-call | tf_op jit(solution)/shard_map/prompt/pallas_call | solution.py:341
  33.4 1.2 %collective-permute-start.10 = (bf16[200,128]{1,0:T(8,128)(2,1)S(1)}, bf16[200,128]{1,0:T(8,128)(2,1)S(1)}, u32[]{:S(2)}, u32[]{:S(2)}) collective-permute-start(bf16[200,128]{1,0:T(8,128)(2,1)S(1)} %get-tuple-element.36), channel_id=1, source_target_pairs={{0,8},{1,9},{2,10},{3,11},{4,12},{5,13},{6,14},{7,15},{8,0},{9,1},... | collective-permute-start | bytes 153608 | tf_op jit(solution)/shard_map/ppermute | solution.py:466
  34.6 2.8 %collective-permute-start.11 = (bf16[200,128]{1,0:T(8,128)(2,1)S(1)}, bf16[200,128]{1,0:T(8,128)(2,1)S(1)}, u32[]{:S(2)}, u32[]{:S(2)}) collective-permute-start(bf16[200,128]{1,0:T(8,128)(2,1)S(1)} %get-tuple-element.37), channel_id=1, source_target_pairs={{0,12},{1,13},{2,14},{3,15},{4,8},{5,9},{6,10},{7,11},{8,4},{9,5},... | collective-permute-start | bytes 153608 | tf_op jit(solution)/shard_map/ppermute | solution.py:466
  37.4 0.5 %collective-permute-start.9 = (bf16[200,128]{1,0:T(8,128)(2,1)S(1)}, bf16[200,128]{1,0:T(8,128)(2,1)S(1)}, u32[]{:S(2)}, u32[]{:S(2)}) collective-permute-start(bf16[200,128]{1,0:T(8,128)(2,1)S(1)} %get-tuple-element.35), channel_id=1, source_target_pairs={{0,4},{1,5},{2,6},{3,7},{4,0},{5,1},{6,2},{7,3},{8,12},{9,13},{10,... | collective-permute-start | bytes 153608 | tf_op jit(solution)/shard_map/ppermute | solution.py:466
  37.8 0.7 %collective-permute-done.10.refs_2_ = bf16[200,128]{1,0:T(8,128)(2,1)S(1)} collective-permute-done((bf16[200,128]{1,0:T(8,128)(2,1)S(1)}, bf16[200,128]{1,0:T(8,128)(2,1)S(1)}, u32[]{:S(2)}, u32[]{:S(2)}) %collective-permute-start.10) | collective-permute-done | bytes 51232 | tf_op jit(solution)/shard_map/ppermute | solution.py:466
  38.5 2.0 %collective-permute-done.11.refs_3_ = bf16[200,128]{1,0:T(8,128)(2,1)S(1)} collective-permute-done((bf16[200,128]{1,0:T(8,128)(2,1)S(1)}, bf16[200,128]{1,0:T(8,128)(2,1)S(1)}, u32[]{:S(2)}, u32[]{:S(2)}) %collective-permute-start.11) | collective-permute-done | bytes 51232 | tf_op jit(solution)/shard_map/ppermute | solution.py:466
  40.5 1.0 %collective-permute-done.9.refs_1_ = bf16[200,128]{1,0:T(8,128)(2,1)S(1)} collective-permute-done((bf16[200,128]{1,0:T(8,128)(2,1)S(1)}, bf16[200,128]{1,0:T(8,128)(2,1)S(1)}, u32[]{:S(2)}, u32[]{:S(2)}) %collective-permute-start.9) | collective-permute-done | bytes 51232 | tf_op jit(solution)/shard_map/ppermute | solution.py:466
  41.5 0.2 merge.1
  41.7 0.1 collective-permute-start.12
  41.7 1.2 %collective-permute-start.13 = (bf16[56,128]{1,0:T(8,128)(2,1)S(1)}, bf16[56,128]{1,0:T(8,128)(2,1)S(1)}, u32[]{:S(2)}, u32[]{:S(2)}) collective-permute-start(bf16[56,128]{1,0:T(8,128)(2,1)S(1)} %get-tuple-element.40), channel_id=1, source_target_pairs={{0,2},{1,3},{2,0},{3,1},{4,6},{5,7},{6,4},{7,5},{8,10},{9,11},{10,... | collective-permute-start | bytes 43016 | tf_op jit(solution)/shard_map/ppermute | solution.py:466
  42.9 0.7 %collective-permute-start.14 = (bf16[56,128]{1,0:T(8,128)(2,1)S(1)}, bf16[56,128]{1,0:T(8,128)(2,1)S(1)}, u32[]{:S(2)}, u32[]{:S(2)}) collective-permute-start(bf16[56,128]{1,0:T(8,128)(2,1)S(1)} %get-tuple-element.41), channel_id=1, source_target_pairs={{0,3},{1,2},{2,1},{3,0},{4,7},{5,6},{6,5},{7,4},{8,11},{9,10},{10,... | collective-permute-start | bytes 43016 | tf_op jit(solution)/shard_map/ppermute | solution.py:466
  43.6 3.1 %suffix.3 = (f32[128,128]{1,0:T(8,128)S(1)}, f32[128,128]{1,0:T(8,128)S(1)}, f32[128,128]{1,0:T(8,128)S(1)}) custom-call(s32[8,128]{1,0:T(8,128)S(1)} %get-tuple-element.28.live_ref, bf16[192,128]{1,0:T(8,128)(2,1)S(1)} %get-tuple-element.29.q_ref, bf16[3,512,2048]{2,1,0:T(8,128)(2,1)} %cache_ref.5), custom_call_target="tpu_custom_call" | custom-call | flops 268435456 | bytes 4194304 | tf_op jit(solution)/shard_map/suffix/pallas_call | solution.py:239
  46.7 0.0 collective-permute-done.12.refs_1_
  46.7 0.0 collective-permute-done.13.refs_2_
  46.7 0.0 collective-permute-done.14.refs_3_
  46.7 0.0 copy-done
  46.7 0.9 %finish.1 = (bf16[3,8192]{1,0:T(4,128)(2,1)}, f32[3]{0:T(128)}) custom-call(bf16[56,128]{1,0:T(8,128)(2,1)S(1)} %get-tuple-element.38.refs_0_, bf16[56,128]{1,0:T(8,128)(2,1)S(1)} %collective-permute-done.12.refs_1_, bf16[56,128]{1,0:T(8,128)(2,1)S(1)} %collective-permute-done.13.refs_2_, bf16[56,128]{1,0:T(8,128)(2,1)S(1)} %collective-permute-done.14.refs_3_, ...), custom_call_target="tpu_custom_call" | custom-call | tf_op jit(solution)/shard_map/finish/pallas_call | solution.py:443
  (1 shorter events, 0.0 us)
Async XLA Ops:
  1.8 44.9 %copy-start = (f32[8192]{0:T(1024)S(1)}, f32[8192]{0:T(1024)}, u32[]{:S(2)}) copy-start(f32[8192]{0:T(1024)} %param.11) | copy-start | bytes 98308
  4.1 28.3 %collective-permute-start.6 = (bf16[2,2,128,256]{3,2,1,0:T(8,128)(2,1)S(1)}, bf16[2,2,128,256]{3,2,1,0:T(8,128)(2,1)S(1)}, u32[]{:S(2)}, u32[]{:S(2)}) collective-permute-start(bf16[2,2,128,256]{3,2,1,0:T(8,128)(2,1)S(1)} %get-tuple-element.31), channel_id=1, source_target_pairs={{0,1},{1,0},{2,3},{3,2},{4,5},{5,4},{6,7},{7,6},{8,9},{9,8},{10,11... | collective-permute-start | bytes 786440 | tf_op jit(solution)/shard_map/ppermute | solution.py:466
  4.6 27.7 %collective-permute-start.7 = (bf16[2,2,128,256]{3,2,1,0:T(8,128)(2,1)S(1)}, bf16[2,2,128,256]{3,2,1,0:T(8,128)(2,1)S(1)}, u32[]{:S(2)}, u32[]{:S(2)}) collective-permute-start(bf16[2,2,128,256]{3,2,1,0:T(8,128)(2,1)S(1)} %get-tuple-element.32), channel_id=1, source_target_pairs={{0,2},{1,3},{2,0},{3,1},{4,6},{5,7},{6,4},{7,5},{8,10},{9,11},{10,... | collective-permute-start | bytes 786440 | tf_op jit(solution)/shard_map/ppermute | solution.py:466
  7.2 25.1 %collective-permute-start.8 = (bf16[2,2,128,256]{3,2,1,0:T(8,128)(2,1)S(1)}, bf16[2,2,128,256]{3,2,1,0:T(8,128)(2,1)S(1)}, u32[]{:S(2)}, u32[]{:S(2)}) collective-permute-start(bf16[2,2,128,256]{3,2,1,0:T(8,128)(2,1)S(1)} %get-tuple-element.33), channel_id=1, source_target_pairs={{0,3},{1,2},{2,1},{3,0},{4,7},{5,6},{6,5},{7,4},{8,11},{9,10},{10,... | collective-permute-start | bytes 786440 | tf_op jit(solution)/shard_map/ppermute | solution.py:466
  7.2 13.1 %collective-permute-start.1 = (bf16[112,128]{1,0:T(8,128)(2,1)S(1)}, bf16[112,128]{1,0:T(8,128)(2,1)S(1)}, u32[]{:S(2)}, u32[]{:S(2)}) collective-permute-start(bf16[112,128]{1,0:T(8,128)(2,1)S(1)} %get-tuple-element.27), channel_id=1, source_target_pairs={{0,2},{1,3},{2,0},{3,1},{4,6},{5,7},{6,4},{7,5},{8,10},{9,11},{10,... | collective-permute-start | bytes 86024 | tf_op jit(solution)/shard_map/ppermute | solution.py:466
  20.3 1.4 %collective-permute-start.2 = (bf16[112,128]{1,0:T(8,128)(2,1)S(1)}, bf16[112,128]{1,0:T(8,128)(2,1)S(1)}, u32[]{:S(2)}, u32[]{:S(2)}) collective-permute-start(bf16[112,128]{1,0:T(8,128)(2,1)S(1)} %collective-permute-done.1.far_ref), channel_id=1, source_target_pairs={{0,1},{1,0},{2,3},{3,2},{4,5},{5,4},{6,7},{7,6},{8,9},{9,8},{10,11... | collective-permute-start | bytes 86024 | tf_op jit(solution)/shard_map/ppermute | solution.py:466
  20.3 1.3 %collective-permute-start = (bf16[56,128]{1,0:T(8,128)(2,1)S(1)}, bf16[56,128]{1,0:T(8,128)(2,1)S(1)}, u32[]{:S(2)}, u32[]{:S(2)}) collective-permute-start(bf16[56,128]{1,0:T(8,128)(2,1)S(1)} %get-tuple-element.26), channel_id=1, source_target_pairs={{0,1},{1,0},{2,3},{3,2},{4,5},{5,4},{6,7},{7,6},{8,9},{9,8},{10,11... | collective-permute-start | bytes 43016 | tf_op jit(solution)/shard_map/ppermute | solution.py:466
  21.7 4.5 %collective-permute-start.3 = (bf16[200,128]{1,0:T(8,128)(2,1)S(1)}, bf16[200,128]{1,0:T(8,128)(2,1)S(1)}, u32[]{:S(2)}, u32[]{:S(2)}) collective-permute-start(bf16[200,128]{1,0:T(8,128)(2,1)S(1)} %pack.1.refs_0_), channel_id=1, source_target_pairs={{0,4},{1,5},{2,6},{3,7},{4,0},{5,1},{6,2},{7,3},{8,12},{9,13},{10,... | collective-permute-start | bytes 153608 | tf_op jit(solution)/shard_map/ppermute | solution.py:466
  23.6 6.7 %collective-permute-start.4 = (bf16[200,128]{1,0:T(8,128)(2,1)S(1)}, bf16[200,128]{1,0:T(8,128)(2,1)S(1)}, u32[]{:S(2)}, u32[]{:S(2)}) collective-permute-start(bf16[200,128]{1,0:T(8,128)(2,1)S(1)} %pack.1.refs_0_), channel_id=1, source_target_pairs={{0,8},{1,9},{2,10},{3,11},{4,12},{5,13},{6,14},{7,15},{8,0},{9,1},... | collective-permute-start | bytes 153608 | tf_op jit(solution)/shard_map/ppermute | solution.py:466
  26.2 6.2 %collective-permute-start.5 = (bf16[200,128]{1,0:T(8,128)(2,1)S(1)}, bf16[200,128]{1,0:T(8,128)(2,1)S(1)}, u32[]{:S(2)}, u32[]{:S(2)}) collective-permute-start(bf16[200,128]{1,0:T(8,128)(2,1)S(1)} %pack.1.refs_0_), channel_id=1, source_target_pairs={{0,12},{1,13},{2,14},{3,15},{4,8},{5,9},{6,10},{7,11},{8,4},{9,5},... | collective-permute-start | bytes 153608 | tf_op jit(solution)/shard_map/ppermute | solution.py:466
  33.4 5.1 %collective-permute-start.10 = (bf16[200,128]{1,0:T(8,128)(2,1)S(1)}, bf16[200,128]{1,0:T(8,128)(2,1)S(1)}, u32[]{:S(2)}, u32[]{:S(2)}) collective-permute-start(bf16[200,128]{1,0:T(8,128)(2,1)S(1)} %get-tuple-element.36), channel_id=1, source_target_pairs={{0,8},{1,9},{2,10},{3,11},{4,12},{5,13},{6,14},{7,15},{8,0},{9,1},... | collective-permute-start | bytes 153608 | tf_op jit(solution)/shard_map/ppermute | solution.py:466
  34.6 5.9 %collective-permute-start.11 = (bf16[200,128]{1,0:T(8,128)(2,1)S(1)}, bf16[200,128]{1,0:T(8,128)(2,1)S(1)}, u32[]{:S(2)}, u32[]{:S(2)}) collective-permute-start(bf16[200,128]{1,0:T(8,128)(2,1)S(1)} %get-tuple-element.37), channel_id=1, source_target_pairs={{0,12},{1,13},{2,14},{3,15},{4,8},{5,9},{6,10},{7,11},{8,4},{9,5},... | collective-permute-start | bytes 153608 | tf_op jit(solution)/shard_map/ppermute | solution.py:466
  37.4 4.1 %collective-permute-start.9 = (bf16[200,128]{1,0:T(8,128)(2,1)S(1)}, bf16[200,128]{1,0:T(8,128)(2,1)S(1)}, u32[]{:S(2)}, u32[]{:S(2)}) collective-permute-start(bf16[200,128]{1,0:T(8,128)(2,1)S(1)} %get-tuple-element.35), channel_id=1, source_target_pairs={{0,4},{1,5},{2,6},{3,7},{4,0},{5,1},{6,2},{7,3},{8,12},{9,13},{10,... | collective-permute-start | bytes 153608 | tf_op jit(solution)/shard_map/ppermute | solution.py:466
  41.7 5.0 %collective-permute-start.12 = (bf16[56,128]{1,0:T(8,128)(2,1)S(1)}, bf16[56,128]{1,0:T(8,128)(2,1)S(1)}, u32[]{:S(2)}, u32[]{:S(2)}) collective-permute-start(bf16[56,128]{1,0:T(8,128)(2,1)S(1)} %get-tuple-element.39), channel_id=1, source_target_pairs={{0,1},{1,0},{2,3},{3,2},{4,5},{5,4},{6,7},{7,6},{8,9},{9,8},{10,11... | collective-permute-start | bytes 43016 | tf_op jit(solution)/shard_map/ppermute | solution.py:466
  41.7 5.0 %collective-permute-start.13 = (bf16[56,128]{1,0:T(8,128)(2,1)S(1)}, bf16[56,128]{1,0:T(8,128)(2,1)S(1)}, u32[]{:S(2)}, u32[]{:S(2)}) collective-permute-start(bf16[56,128]{1,0:T(8,128)(2,1)S(1)} %get-tuple-element.40), channel_id=1, source_target_pairs={{0,2},{1,3},{2,0},{3,1},{4,6},{5,7},{6,4},{7,5},{8,10},{9,11},{10,... | collective-permute-start | bytes 43016 | tf_op jit(solution)/shard_map/ppermute | solution.py:466
  42.9 3.8 %collective-permute-start.14 = (bf16[56,128]{1,0:T(8,128)(2,1)S(1)}, bf16[56,128]{1,0:T(8,128)(2,1)S(1)}, u32[]{:S(2)}, u32[]{:S(2)}) collective-permute-start(bf16[56,128]{1,0:T(8,128)(2,1)S(1)} %get-tuple-element.41), channel_id=1, source_target_pairs={{0,3},{1,2},{2,1},{3,0},{4,7},{5,6},{6,5},{7,4},{8,11},{9,10},{10,... | collective-permute-start | bytes 43016 | tf_op jit(solution)/shard_map/ppermute | solution.py:466
